TPU v7x, 256 devices: a whole 4x4x8 slice. The times are simulated.
256 devices in a mesh: dp: 16 (over x, y), expert: 16 (over z, core).
Axes of the slice: x: 4, y: 4, z: 8, core: 2. Of those that a mesh axis runs over, the one named last changes fastest.
Arguments:
- hidden: bfloat16 [16, 16, 384, 1024], P('dp', 'expert'), may hold values from -6 to 6
- down_weight: bfloat16 [16, 1024, 3584], P('expert'), may hold values from -0.1875 to 0.1875
- cotangent: bfloat16 [8192, 3584], P('dp', 'expert'), may hold values from -6 to 6
- expert_ids: int32 [8192, 8], P('dp'), may hold values from 0 to 15, as said below
- gate_weights: bfloat16 [8192, 8], P('dp'), may hold values from 0.049804688 to 0.5
- row_token: int32 [16, 16, 384], P('dp', 'expert'), may hold values from -1 to 511, as said below
- tile_count: int32 [16, 16], P('dp', 'expert'), may hold values from 1 to 3, as said below
Outputs:
- mixed_out: bfloat16 [8192, 3584], P('dp', 'expert')
- hidden_grad: bfloat16 [16, 16, 384, 1024], P('dp', 'expert')
- weight_grad: float32 [16, 1024, 3584], P('expert', 'dp')
Inputs may be any that keep to these rules, and one draw needn't show every extreme that they name: `expert_ids`: each token names 8 different experts; every expert is named by some token of every group. row_token[i, e, r] is the index within group i (0 to 511) of a token that names expert e, or -1 for an empty slot; each token of a group stands exactly once in the rows of each expert it names and nowhere else; an expert's filled rows come first. tile_count[i, e] is the number of 128-row tiles that hold expert e's filled rows in group i, except for one expert of every group whose count is one tile less; the busiest expert of every group has 384 filled rows, all of them counted.
All inputs are finite; a program needn't handle non-finite values.
Results may differ from a plain program's by a relative error of at most 0.013.
Values may be sent and summed in bfloat16 or wider, within the bound.
A program may use at most 128 MiB of HBM per device.

v0:
```python
import jax
import jax.numpy as jnp
from jax import lax
from jax.sharding import PartitionSpec as P

EXPERTS = 16
TILE = 128


def swapped(shard, axis, bit):
    return lax.ppermute(shard, axis, [(i, i ^ 1 << bit) for i in range(lax.axis_size(axis))])


def tile_products(rows_in, weight_mat, count, contract_dim):
    rows_cap = rows_in.shape[0]
    width_out = weight_mat.shape[1 - contract_dim]

    def one_tile(tile_index, outputs):
        block = lax.dynamic_slice_in_dim(rows_in, tile_index * TILE, TILE, 0)
        product = lax.dot_general(
            block,
            weight_mat,
            (((1,), (contract_dim,)), ((), ())),
            preferred_element_type=jnp.float32,
        )
        return lax.dynamic_update_slice_in_dim(
            outputs, product.astype(jnp.bfloat16), tile_index * TILE, 0
        )

    return lax.fori_loop(0, count, one_tile, jnp.zeros((rows_cap, width_out), jnp.bfloat16))


def body(hidden, down_weight, cotangent, expert_ids, gate_weights, row_token, tile_count):
    local_count = down_weight.shape[0]
    group_size = cotangent.shape[0]
    expert_index = jnp.arange(EXPERTS, dtype=jnp.int32)
    named_cols = expert_ids[:, :, None] == expert_index[None, None, :]
    gate_cols = jnp.sum(
        jnp.where(named_cols, gate_weights[:, :, None].astype(jnp.float32), 0.0), axis=1
    ).astype(jnp.bfloat16)
    group_cot = lax.all_gather(cotangent, "expert", axis=1, tiled=True)
    width = group_cot.shape[1]
    first_expert = lax.axis_index("expert") * local_count
    slot_index = jnp.arange(hidden.shape[2], dtype=jnp.int32)
    share_rows = down_weight.shape[1] // lax.axis_size("dp")
    partial_value = jnp.zeros((group_size, width), jnp.float32)
    token_rows = row_token[0, 0]
    count = tile_count[0, 0]
    live_rows = (token_rows >= 0) & (slot_index < count * TILE)
    safe_rows = jnp.where(live_rows, token_rows, 0)
    column = lax.dynamic_index_in_dim(gate_cols, first_expert + 0, 1, keepdims=False)
    row_gate = jnp.where(live_rows, column[safe_rows].astype(jnp.float32), 0.0)
    target = jnp.where(live_rows, token_rows, group_size)
    hidden_rows = hidden[0, 0]
    weight_mat = down_weight[0]
    out_rows = tile_products(hidden_rows, weight_mat, count, 0)
    partial_value = partial_value.at[target].add(
        row_gate[:, None] * out_rows.astype(jnp.float32), mode="drop"
    )
    routed = (row_gate[:, None] * group_cot[safe_rows].astype(jnp.float32)).astype(jnp.bfloat16)
    grad_list = [tile_products(routed, weight_mat, count, 1)]

    def weight_rows(start, rows_count, hidden_rows=hidden_rows, routed_rows=routed):
        return lax.dot_general(
            hidden_rows, routed_rows, (((0,), (0,)), ((), ())), preferred_element_type=jnp.float32
        )

    weight_list = [
        lax.psum_scatter(
            weight_rows(jnp.int32(0), share_rows * lax.axis_size("dp")).astype(jnp.bfloat16),
            "dp",
            scatter_dimension=0,
            tiled=True,
        ).astype(jnp.float32)
    ]
    merged = partial_value
    top_bit = lax.axis_size("expert").bit_length() - 1
    axis_index = lax.axis_index("expert")
    for bit_index in reversed(range(top_bit)):
        half_cols = merged.shape[1] // 2
        lower_half = merged[:, :half_cols]
        upper_half = merged[:, half_cols:]
        high_side = axis_index // 2**bit_index % 2 == 1
        sending = jnp.where(high_side, lower_half, upper_half)
        keeping = jnp.where(high_side, upper_half, lower_half)
        merged = keeping + swapped(sending.astype(jnp.bfloat16), "expert", bit_index).astype(
            sending.dtype
        )
    mixed_out = merged.astype(jnp.bfloat16)
    hidden_grad = jnp.stack(grad_list, axis=0)[None]
    weight_grad = jnp.stack(weight_list, axis=0)
    return (mixed_out, hidden_grad, weight_grad)


def solution(mesh):
    placed = (
        P("dp", "expert", None, None),
        P("expert", None, None),
        P("dp", "expert"),
        P("dp", None),
        P("dp", None),
        P("dp", "expert", None),
        P("dp", "expert"),
    )
    return jax.shard_map(
        body,
        mesh=mesh,
        in_specs=placed,
        out_specs=(P("dp", "expert"), P("dp", "expert", None, None), P("expert", "dp", None)),
        check_vma=False,
    )
```

profile of v0, /device:TPU:1, one launch (start us, length us, event | category | flops | bytes accessed | tf_op | source)
XLA Modules:
  0.0 314.3 jit_solution(3200420147319569231)
XLA Ops:
  10.8 2.8 gather_fusion
  14.3 41.0 %all-gather.2.cloned.1.call-done = bf16[512,3584]{0,1:T(8,128)(2,1)} async-done(((bf16[512,224]{0,1:T(8,128)(2,1)}), bf16[512,3584]{0,1:T(8,128)(2,1)}) %all-gather.2.cloned.1.call-update) | async-done | bytes 3670032 | tf_op jit(solution)/shard_map/all_gather | solution.py:41
  55.3 6.0 %copy.24 = bf16[512,3584]{1,0:T(8,128)(2,1)} copy(bf16[512,3584]{0,1:T(8,128)(2,1)} %all-gather.2.cloned.1.call-done) | data formatting | bytes 7340032 | tf_op jit(solution)/shard_map/all_gather | solution.py:41
  61.3 10.1 %gather_fusion.1 = bf16[384,3584]{1,0:T(8,128)(2,1)} fusion(bf16[512,3584]{1,0:T(8,128)(2,1)} %copy.24, s32[1024]{0:T(1024)S(1)} %pad_clamp_fusion), kind=kCustom, calls=%fused_computation.1 | custom fusion | bytes 5506560 | tf_op jit(solution)/shard_map/gather | solution.py:60
  71.4 2.6 multiply_convert_fusion
  74.1 6.2 %fusion.6 = bf16[1024,3584]{0,1:T(8,128)(2,1)} fusion(bf16[384,3584]{1,0:T(8,128)(2,1)S(1)} %multiply_convert_fusion, bf16[1,1,384,1024]{3,2,1,0:T(8,128)(2,1)S(1)} %copy-done.3), kind=kOutput, calls=%fused_computation.12 | convolution fusion | flops 2822242304 | bytes 10878976 | tf_op jit(solution)/shard_map/dot_general | solution.py:64
  80.2 10.0 %copy.27 = bf16[1024,3584]{1,0:T(8,128)(2,1)} copy(bf16[1024,3584]{0,1:T(8,128)(2,1)} %fusion.6) | data formatting | bytes 14680064
  92.0 18.8 %while.20 = (s32[]{:T(128)}, bf16[384,3584]{1,0:T(8,128)(2,1)}, s32[]{:T(128)}, bf16[384,1024]{1,0:T(8,128)(2,1)S(1)}, bf16[1024,3584]{1,0:T(8,128)(2,1)}, /*index=5*/s32[]{:T(128)}, s32[]{:T(128)}, s32[]{:T(128)}, s32[]{:T(128)}) while((s32[]{:T(128)}, bf16[384,3584]{1,0:T(8,128)(2,1)}, s32[]{:T(128)}, bf16[384,1024]{1,0:T(8,128)(2,1)S(1)}, ...), condition=%wide.region_2.3_spmd, body=%wide.region_1.2_spmd.sunk | while | flops 939982848 | bytes 8520843 | solution.py:30
  92.7 5.1 %fusion.28 = bf16[384,3584]{1,0:T(8,128)(2,1)} fusion(bf16[384,3584]{1,0:T(8,128)(2,1)} %get-tuple-element.169, s32[]{:T(128)S(6)} %select_n.202, bf16[1024,3584]{1,0:T(8,128)(2,1)} %get-tuple-element.181, bf16[384,1024]{1,0:T(8,128)(2,1)S(1)} %get-tuple-element.180), kind=kOutput, calls=%fused_computation.4.clone.1 | convolution fusion | flops 939982848 | bytes 8520704 | tf_op jit(solution)/shard_map/while/body/dot_general | solution.py:20
  98.5 5.5 %fusion.28 = bf16[384,3584]{1,0:T(8,128)(2,1)} fusion(bf16[384,3584]{1,0:T(8,128)(2,1)} %get-tuple-element.169, s32[]{:T(128)S(6)} %select_n.202, bf16[1024,3584]{1,0:T(8,128)(2,1)} %get-tuple-element.181, bf16[384,1024]{1,0:T(8,128)(2,1)S(1)} %get-tuple-element.180), kind=kOutput, calls=%fused_computation.4.clone.1 | convolution fusion | flops 939982848 | bytes 8520704 | tf_op jit(solution)/shard_map/while/body/dot_general | solution.py:20
  104.6 5.3 %fusion.28 = bf16[384,3584]{1,0:T(8,128)(2,1)} fusion(bf16[384,3584]{1,0:T(8,128)(2,1)} %get-tuple-element.169, s32[]{:T(128)S(6)} %select_n.202, bf16[1024,3584]{1,0:T(8,128)(2,1)} %get-tuple-element.181, bf16[384,1024]{1,0:T(8,128)(2,1)S(1)} %get-tuple-element.180), kind=kOutput, calls=%fused_computation.4.clone.1 | convolution fusion | flops 939982848 | bytes 8520704 | tf_op jit(solution)/shard_map/while/body/dot_general | solution.py:20
  110.8 12.9 %scatter_custom_fusion = f32[512,3584]{1,0:T(8,128)} fusion(s32[384]{0:T(512)S(1)} %get-tuple-element.74, bf16[384,3584]{1,0:T(8,128)(2,1)} %get-tuple-element.59, f32[]{:T(128)} %constant.98.clone.1, f32[384]{0:T(512)S(1)} %convert_select_fusion), kind=kCustom, calls=%fused_computation.14 | custom fusion | flops 4128768 | bytes 10094596 | tf_op jit(solution)/shard_map/scatter-add | solution.py:57
  123.6 4.9 %select_convert_fusion = bf16[512,1792]{1,0:T(8,128)(2,1)} fusion(f32[512,3584]{1,0:T(8,128)} %scatter_custom_fusion, pred[]{:T(512)S(6)} %eq.33), kind=kLoop, calls=%fused_computation.18 | loop fusion | flops 917504 | bytes 5505025 | tf_op jit(solution)/shard_map/convert_element_type | solution.py:86
  128.6 80.4 %collective-permute-done = bf16[512,1792]{1,0:T(8,128)(2,1)} collective-permute-done((bf16[512,1792]{1,0:T(8,128)(2,1)}, bf16[512,1792]{1,0:T(8,128)(2,1)}, u32[]{:S(2)}, u32[]{:S(2)}) %collective-permute-start) | collective-permute-done | bytes 1835040 | tf_op jit(solution)/shard_map/ppermute | solution.py:11
  209.0 4.3 %convert_add_fusion = f32[512,1792]{1,0:T(8,128)S(1)} fusion(bf16[512,1792]{1,0:T(8,128)(2,1)} %collective-permute-done, f32[512,3584]{1,0:T(8,128)} %scatter_custom_fusion, pred[]{:T(512)S(6)} %eq.33), kind=kLoop, calls=%fused_computation.17 | loop fusion | flops 2752512 | bytes 12845057 | tf_op jit(solution)/shard_map/add | solution.py:86
  213.2 1.9 copy-done
  216.2 43.0 %collective-permute-done.1 = bf16[512,896]{1,0:T(8,128)(2,1)} collective-permute-done((bf16[512,896]{1,0:T(8,128)(2,1)}, bf16[512,896]{1,0:T(8,128)(2,1)}, u32[]{:S(2)}, u32[]{:S(2)}) %collective-permute-start.1) | collective-permute-done | bytes 917536 | tf_op jit(solution)/shard_map/ppermute | solution.py:11
  259.2 2.6 convert_add_fusion.1
  263.6 13.1 %collective-permute-done.2 = bf16[512,448]{1,0:T(8,128)(2,1)} collective-permute-done((bf16[512,448]{1,0:T(8,128)(2,1)S(1)}, bf16[512,448]{1,0:T(8,128)(2,1)}, u32[]{:S(2)}, u32[]{:S(2)}) %collective-permute-start.2) | collective-permute-done | bytes 458784 | tf_op jit(solution)/shard_map/ppermute | solution.py:11
  276.7 2.0 convert_add_fusion.2
  284.9 19.3 %while.21 = (s32[]{:T(128)}, bf16[384,1024]{1,0:T(8,128)(2,1)S(1)}, s32[]{:T(128)}, bf16[384,3584]{1,0:T(8,128)(2,1)S(1)}, bf16[1024,3584]{1,0:T(8,128)(2,1)}, /*index=5*/s32[]{:T(128)}, s32[]{:T(128)}, s32[]{:T(128)}, s32[]{:T(128)}) while((s32[]{:T(128)}, bf16[384,1024]{1,0:T(8,128)(2,1)S(1)}, s32[]{:T(128)}, ...), condition=%wide.region_5.6_spmd, body=%wide.region_4.5_spmd.sunk | while | flops 939655168 | bytes 8520843 | solution.py:30
  285.5 5.5 %fusion.31 = bf16[384,1024]{1,0:T(8,128)(2,1)S(1)} fusion(bf16[384,1024]{1,0:T(8,128)(2,1)S(1)} %get-tuple-element.196, s32[]{:T(128)S(6)} %select_n.203, bf16[1024,3584]{1,0:T(8,128)(2,1)} %get-tuple-element.208, bf16[384,3584]{1,0:T(8,128)(2,1)S(1)} %get-tuple-element.207), kind=kOutput, calls=%fused_computation.8.clone.1 | convolution fusion | flops 939655168 | bytes 8520704 | tf_op jit(solution)/shard_map/while/body/dot_general | solution.py:20
  291.7 5.5 %fusion.31 = bf16[384,1024]{1,0:T(8,128)(2,1)S(1)} fusion(bf16[384,1024]{1,0:T(8,128)(2,1)S(1)} %get-tuple-element.196, s32[]{:T(128)S(6)} %select_n.203, bf16[1024,3584]{1,0:T(8,128)(2,1)} %get-tuple-element.208, bf16[384,3584]{1,0:T(8,128)(2,1)S(1)} %get-tuple-element.207), kind=kOutput, calls=%fused_computation.8.clone.1 | convolution fusion | flops 939655168 | bytes 8520704 | tf_op jit(solution)/shard_map/while/body/dot_general | solution.py:20
  297.9 5.5 %fusion.31 = bf16[384,1024]{1,0:T(8,128)(2,1)S(1)} fusion(bf16[384,1024]{1,0:T(8,128)(2,1)S(1)} %get-tuple-element.196, s32[]{:T(128)S(6)} %select_n.203, bf16[1024,3584]{1,0:T(8,128)(2,1)} %get-tuple-element.208, bf16[384,3584]{1,0:T(8,128)(2,1)S(1)} %get-tuple-element.207), kind=kOutput, calls=%fused_computation.8.clone.1 | convolution fusion | flops 939655168 | bytes 8520704 | tf_op jit(solution)/shard_map/while/body/dot_general | solution.py:20
  (36 shorter events, 17.7 us)
Async XLA Ops:
  7.2 48.1 %all-gather.2.cloned.1.call-start = ((), (), s32[]{:S(2)}) async-start(), calls=%async_computation.1 | async-start | bytes 3899392 | tf_op jit(solution)/shard_map/all_gather | solution.py:41
  7.9 296.3 %reduce-scatter.4.cloned.1.call-start = ((), (), s32[]{:S(2)}) async-start(), calls=%async_computation.2 | async-start | bytes 7798784
  71.4 2.7 copy-start.3
  128.6 80.4 %collective-permute-start = (bf16[512,1792]{1,0:T(8,128)(2,1)}, bf16[512,1792]{1,0:T(8,128)(2,1)}, u32[]{:S(2)}, u32[]{:S(2)}) collective-permute-start(bf16[512,1792]{1,0:T(8,128)(2,1)} %select_convert_fusion), channel_id=1, source_target_pairs={{0,8},{1,9},{2,10},{3,11},{4,12},{5,13},{6,14},{7,15},{8,0},{9,1},... | collective-permute-start | bytes 5505032 | tf_op jit(solution)/shard_map/ppermute | solution.py:11
  213.2 1.9 copy-start
  216.2 43.0 %collective-permute-start.1 = (bf16[512,896]{1,0:T(8,128)(2,1)}, bf16[512,896]{1,0:T(8,128)(2,1)}, u32[]{:S(2)}, u32[]{:S(2)}) collective-permute-start(bf16[512,896]{1,0:T(8,128)(2,1)} %select_convert_fusion.1), channel_id=1, source_target_pairs={{0,4},{1,5},{2,6},{3,7},{4,0},{5,1},{6,2},{7,3},{8,12},{9,13},{10,... | collective-permute-start | bytes 2752520 | tf_op jit(solution)/shard_map/ppermute | solution.py:11
  261.8 1.3 copy-start.1
  263.3 13.4 %collective-permute-start.2 = (bf16[512,448]{1,0:T(8,128)(2,1)S(1)}, bf16[512,448]{1,0:T(8,128)(2,1)}, u32[]{:S(2)}, u32[]{:S(2)}) collective-permute-start(bf16[512,448]{1,0:T(8,128)(2,1)S(1)} %select_convert_fusion.2), channel_id=1, source_target_pairs={{0,2},{1,3},{2,0},{3,1},{4,6},{5,7},{6,4},{7,5},{8,10},{9,11},{10,... | collective-permute-start | bytes 1376264 | tf_op jit(solution)/shard_map/ppermute | solution.py:11
  278.7 1.0 copy-start.2
  279.9 2.6 collective-permute-start.3
  304.1 3.3 %copy-start.4 = (bf16[384,1024]{1,0:T(8,128)(2,1)}, bf16[384,1024]{1,0:T(8,128)(2,1)S(1)}, u32[]{:S(2)}) copy-start(bf16[384,1024]{1,0:T(8,128)(2,1)S(1)} %get-tuple-element.60) | copy-start | bytes 2359300
Sparse Core Ops, SparseCore 0:
  9.8 45.4 all-gather.1
  90.4 85.8 reduce-scatter.3
where the time goes:
time: 315 us; the launch traced here: 314 us
  waiting for transfers between devices  179 us (57%)
  local copies, waits for them, and re-layouts  38.9 us (12%)
  matrix products  38.7 us (12%)
  other arithmetic  35.2 us (11%)
  between operations  14.9 us (5%)
  loops' own time  5.51 us (2%)
    ppermute x4, waiting for transfers between devices, swapped(): lax.ppermute(shard, axis, [(i, i ^ 1 << bit) for i in range(lax.axis_size...  138 us
    all_gather x1, waiting for transfers between devices, body(): group_cot = lax.all_gather(cotangent, 'expert', axis=1, tiled=True)  41 us
    dot_general x6, matrix products, one_tile(): lax.dot_general(block, weight_mat, (((1,), (contract_dim,)), ((), ())), p...  32.5 us
    unnamed x14, local copies, waits for them, and re-layouts  18.2 us
    scatter-add x1, other arithmetic, body(): partial_value.at[target]  12.9 us
    gather x1, local copies, waits for them, and re-layouts, body(): group_cot[safe_rows].astype(jnp.float32)  10.1 us
    add x3, other arithmetic, body(): keeping + swapped(sending.astype(jnp.bfloat16), 'expert', bit_index).asty...  8.84 us
    convert_element_type x4, other arithmetic, body(): sending.astype(jnp.bfloat16)  6.37 us
  transfers between devices with their start and end apart: 6, of which 5 were waited for; matrix products, arithmetic and copies ran while one was open for 22% of the time, Pallas kernels for 0%

commit v1 on v0

--- a/solution.py
+++ b/solution.py
@@ -38,7 +38,9 @@
     gate_cols = jnp.sum(
         jnp.where(named_cols, gate_weights[:, :, None].astype(jnp.float32), 0.0), axis=1
     ).astype(jnp.bfloat16)
-    group_cot = lax.all_gather(cotangent, "expert", axis=1, tiled=True)
+    group_cot = jnp.concatenate(
+        lax.all_to_all(jnp.stack([cotangent] * lax.axis_size("expert")), "expert", 0, 0), axis=1
+    )
     width = group_cot.shape[1]
     first_expert = lax.axis_index("expert") * local_count
     slot_index = jnp.arange(hidden.shape[2], dtype=jnp.int32)

time: 315 us -> 363 us (1.15)
  waiting for transfers between devices: 179 us -> 215 us
  starting transfers between devices: 1.83 us -> 11.9 us
    all_to_all x0 -> x1, waiting for transfers between devices: none -> 78.6 us  [body(): lax.all_to_all(jnp.stack([cotangent] * lax.axis_size('expert')), 'expert'...]
    all_gather x1 -> x0, waiting for transfers between devices: 41 us -> none  [body(): group_cot = lax.all_gather(cotangent, 'expert', axis=1, tiled=True)]
    all_to_all x0 -> x1, starting transfers between devices: none -> 10.1 us  [body(): lax.all_to_all(jnp.stack([cotangent] * lax.axis_size('expert')), 'expert'...]
    all_gather x1 -> x0, local copies, waits for them, and re-layouts: 5.95 us -> none  [body(): group_cot = lax.all_gather(cotangent, 'expert', axis=1, tiled=True)]
    reshape x0 -> x1, local copies, waits for them, and re-layouts: none -> 5.92 us  [body(): jnp.concatenate(lax.all_to_all(jnp.stack([cotangent] * lax.axis_size('exp...]
    unnamed x14 -> x20, local copies, waits for them, and re-layouts: 18.2 us -> 18.2 us
  transfers between devices with their start and end apart: 6 -> 6, of which waited for: 5 -> 5; matrix products, arithmetic and copies ran while one was open for 22% -> 19% of each run, Pallas kernels for 0% -> 0%
where the time goes in v1:
time: 363 us; the launch traced here: 360 us
  waiting for transfers between devices  215 us (59%)
  local copies, waits for them, and re-layouts  41.9 us (12%)
  matrix products  38.3 us (11%)
  other arithmetic  32.7 us (9%)
  between operations  14.9 us (4%)
  starting transfers between devices  11.9 us (3%)
  loops' own time  5.51 us (2%)
    ppermute x4, waiting for transfers between devices, swapped(): lax.ppermute(shard, axis, [(i, i ^ 1 << bit) for i in range(lax.axis_size...  136 us
    all_to_all x1, waiting for transfers between devices, body(): lax.all_to_all(jnp.stack([cotangent] * lax.axis_size('expert')), 'expert'...  78.6 us
    dot_general x6, matrix products, one_tile(): lax.dot_general(block, weight_mat, (((1,), (contract_dim,)), ((), ())), p...  32.1 us
    unnamed x20, local copies, waits for them, and re-layouts  18.2 us
    scatter-add x1, other arithmetic, body(): partial_value.at[target]  12.8 us
    all_to_all x1, starting transfers between devices, body(): lax.all_to_all(jnp.stack([cotangent] * lax.axis_size('expert')), 'expert'...  10.1 us
    gather x1, local copies, waits for them, and re-layouts, body(): group_cot[safe_rows].astype(jnp.float32)  10.1 us
    add x3, other arithmetic, body(): keeping + swapped(sending.astype(jnp.bfloat16), 'expert', bit_index).asty...  8.84 us
  transfers between devices with their start and end apart: 6, of which 5 were waited for; matrix products, arithmetic and copies ran while one was open for 19% of the time, Pallas kernels for 0%

profile of v1, /device:TPU:1, one launch (start us, length us, event | category | flops | bytes accessed | tf_op | source)
XLA Modules:
  0.0 360.3 jit_solution(10277565753340371572)
XLA Ops:
  7.2 3.1 stack.7
  10.3 10.1 %all-to-all-start = ((bf16[16,512,224]{1,2,0:T(8,128)(2,1)}), bf16[16,512,224]{1,2,0:T(8,128)(2,1)}, u32[]{:S(2)}, u32[]{:S(2)}) async-start(bf16[16,512,224]{1,2,0:T(8,128)(2,1)} %stack.7), calls=%async_computation | async-start | bytes 7340032 | tf_op jit(solution)/shard_map/all_to_all | solution.py:42
  21.2 2.8 gather_fusion
  24.1 78.6 %all-to-all-done = bf16[16,512,224]{1,2,0:T(8,128)(2,1)} async-done(((bf16[16,512,224]{1,2,0:T(8,128)(2,1)}), bf16[16,512,224]{1,2,0:T(8,128)(2,1)}, u32[]{:S(2)}, u32[]{:S(2)}) %all-to-all-start) | async-done | bytes 3670048 | tf_op jit(solution)/shard_map/all_to_all | solution.py:42
  102.7 5.9 %copy.24 = bf16[512,3584]{1,0:T(8,128)(2,1)} copy(bf16[512,3584]{0,1:T(8,128)(2,1)} %bitcast.5) | data formatting | bytes 7340032 | tf_op jit(solution)/shard_map/reshape | solution.py:41
  108.6 10.1 %gather_fusion.1 = bf16[384,3584]{1,0:T(8,128)(2,1)} fusion(bf16[512,3584]{1,0:T(8,128)(2,1)} %copy.24, s32[1024]{0:T(1024)S(1)} %pad_clamp_fusion), kind=kCustom, calls=%fused_computation.1 | custom fusion | bytes 5506560 | tf_op jit(solution)/shard_map/gather | solution.py:62
  118.7 2.6 multiply_convert_fusion
  121.4 6.2 %fusion.6 = bf16[1024,3584]{0,1:T(8,128)(2,1)} fusion(bf16[384,3584]{1,0:T(8,128)(2,1)S(1)} %multiply_convert_fusion, bf16[1,1,384,1024]{3,2,1,0:T(8,128)(2,1)S(1)} %copy-done.3), kind=kOutput, calls=%fused_computation.12 | convolution fusion | flops 2822242304 | bytes 10878976 | tf_op jit(solution)/shard_map/dot_general | solution.py:66
  127.5 10.0 %copy.27 = bf16[1024,3584]{1,0:T(8,128)(2,1)} copy(bf16[1024,3584]{0,1:T(8,128)(2,1)} %fusion.6) | data formatting | bytes 14680064
  139.3 18.4 %while.20 = (s32[]{:T(128)}, bf16[384,3584]{1,0:T(8,128)(2,1)}, s32[]{:T(128)}, bf16[384,1024]{1,0:T(8,128)(2,1)S(1)}, bf16[1024,3584]{1,0:T(8,128)(2,1)}, /*index=5*/s32[]{:T(128)}, s32[]{:T(128)}, s32[]{:T(128)}, s32[]{:T(128)}) while((s32[]{:T(128)}, bf16[384,3584]{1,0:T(8,128)(2,1)}, s32[]{:T(128)}, bf16[384,1024]{1,0:T(8,128)(2,1)S(1)}, ...), condition=%wide.region_2.3_spmd, body=%wide.region_1.2_spmd.sunk | while | flops 939982848 | bytes 8520843 | solution.py:30
  140.0 5.1 %fusion.28 = bf16[384,3584]{1,0:T(8,128)(2,1)} fusion(bf16[384,3584]{1,0:T(8,128)(2,1)} %get-tuple-element.169, s32[]{:T(128)S(6)} %select_n.202, bf16[1024,3584]{1,0:T(8,128)(2,1)} %get-tuple-element.181, bf16[384,1024]{1,0:T(8,128)(2,1)S(1)} %get-tuple-element.180), kind=kOutput, calls=%fused_computation.4.clone.1 | convolution fusion | flops 939982848 | bytes 8520704 | tf_op jit(solution)/shard_map/while/body/dot_general | solution.py:20
  145.8 5.2 %fusion.28 = bf16[384,3584]{1,0:T(8,128)(2,1)} fusion(bf16[384,3584]{1,0:T(8,128)(2,1)} %get-tuple-element.169, s32[]{:T(128)S(6)} %select_n.202, bf16[1024,3584]{1,0:T(8,128)(2,1)} %get-tuple-element.181, bf16[384,1024]{1,0:T(8,128)(2,1)S(1)} %get-tuple-element.180), kind=kOutput, calls=%fused_computation.4.clone.1 | convolution fusion | flops 939982848 | bytes 8520704 | tf_op jit(solution)/shard_map/while/body/dot_general | solution.py:20
  151.6 5.2 %fusion.28 = bf16[384,3584]{1,0:T(8,128)(2,1)} fusion(bf16[384,3584]{1,0:T(8,128)(2,1)} %get-tuple-element.169, s32[]{:T(128)S(6)} %select_n.202, bf16[1024,3584]{1,0:T(8,128)(2,1)} %get-tuple-element.181, bf16[384,1024]{1,0:T(8,128)(2,1)S(1)} %get-tuple-element.180), kind=kOutput, calls=%fused_computation.4.clone.1 | convolution fusion | flops 939982848 | bytes 8520704 | tf_op jit(solution)/shard_map/while/body/dot_general | solution.py:20
  157.7 12.8 %scatter_custom_fusion = f32[512,3584]{1,0:T(8,128)} fusion(s32[384]{0:T(512)S(1)} %get-tuple-element.74, bf16[384,3584]{1,0:T(8,128)(2,1)} %get-tuple-element.59, f32[]{:T(128)} %constant.98.clone.1, f32[384]{0:T(512)S(1)} %convert_select_fusion), kind=kCustom, calls=%fused_computation.14 | custom fusion | flops 4128768 | bytes 10094596 | tf_op jit(solution)/shard_map/scatter-add | solution.py:59
  170.5 5.2 %select_convert_fusion = bf16[512,1792]{1,0:T(8,128)(2,1)} fusion(f32[512,3584]{1,0:T(8,128)} %scatter_custom_fusion, pred[]{:T(512)S(6)} %eq.33), kind=kLoop, calls=%fused_computation.18 | loop fusion | flops 917504 | bytes 5505025 | tf_op jit(solution)/shard_map/convert_element_type | solution.py:88
  175.7 80.9 %collective-permute-done = bf16[512,1792]{1,0:T(8,128)(2,1)} collective-permute-done((bf16[512,1792]{1,0:T(8,128)(2,1)}, bf16[512,1792]{1,0:T(8,128)(2,1)}, u32[]{:S(2)}, u32[]{:S(2)}) %collective-permute-start) | collective-permute-done | bytes 1835040 | tf_op jit(solution)/shard_map/ppermute | solution.py:11
  256.6 4.3 %convert_add_fusion = f32[512,1792]{1,0:T(8,128)S(1)} fusion(bf16[512,1792]{1,0:T(8,128)(2,1)} %collective-permute-done, f32[512,3584]{1,0:T(8,128)} %scatter_custom_fusion, pred[]{:T(512)S(6)} %eq.33), kind=kLoop, calls=%fused_computation.17 | loop fusion | flops 2752512 | bytes 12845057 | tf_op jit(solution)/shard_map/add | solution.py:88
  263.9 41.3 %collective-permute-done.1 = bf16[512,896]{1,0:T(8,128)(2,1)} collective-permute-done((bf16[512,896]{1,0:T(8,128)(2,1)}, bf16[512,896]{1,0:T(8,128)(2,1)}, u32[]{:S(2)}, u32[]{:S(2)}) %collective-permute-start.1) | collective-permute-done | bytes 917536 | tf_op jit(solution)/shard_map/ppermute | solution.py:11
  305.1 2.6 convert_add_fusion.1
  309.6 13.1 %collective-permute-done.2 = bf16[512,448]{1,0:T(8,128)(2,1)} collective-permute-done((bf16[512,448]{1,0:T(8,128)(2,1)S(1)}, bf16[512,448]{1,0:T(8,128)(2,1)}, u32[]{:S(2)}, u32[]{:S(2)}) %collective-permute-start.2) | collective-permute-done | bytes 458784 | tf_op jit(solution)/shard_map/ppermute | solution.py:11
  330.8 19.3 %while.21 = (s32[]{:T(128)}, bf16[384,1024]{1,0:T(8,128)(2,1)S(1)}, s32[]{:T(128)}, bf16[384,3584]{1,0:T(8,128)(2,1)S(1)}, bf16[1024,3584]{1,0:T(8,128)(2,1)}, /*index=5*/s32[]{:T(128)}, s32[]{:T(128)}, s32[]{:T(128)}, s32[]{:T(128)}) while((s32[]{:T(128)}, bf16[384,1024]{1,0:T(8,128)(2,1)S(1)}, s32[]{:T(128)}, ...), condition=%wide.region_5.6_spmd, body=%wide.region_4.5_spmd.sunk | while | flops 939655168 | bytes 8520843 | solution.py:30
  331.5 5.5 %fusion.31 = bf16[384,1024]{1,0:T(8,128)(2,1)S(1)} fusion(bf16[384,1024]{1,0:T(8,128)(2,1)S(1)} %get-tuple-element.196, s32[]{:T(128)S(6)} %select_n.203, bf16[1024,3584]{1,0:T(8,128)(2,1)} %get-tuple-element.208, bf16[384,3584]{1,0:T(8,128)(2,1)S(1)} %get-tuple-element.207), kind=kOutput, calls=%fused_computation.8.clone.1 | convolution fusion | flops 939655168 | bytes 8520704 | tf_op jit(solution)/shard_map/while/body/dot_general | solution.py:20
  337.7 5.5 %fusion.31 = bf16[384,1024]{1,0:T(8,128)(2,1)S(1)} fusion(bf16[384,1024]{1,0:T(8,128)(2,1)S(1)} %get-tuple-element.196, s32[]{:T(128)S(6)} %select_n.203, bf16[1024,3584]{1,0:T(8,128)(2,1)} %get-tuple-element.208, bf16[384,3584]{1,0:T(8,128)(2,1)S(1)} %get-tuple-element.207), kind=kOutput, calls=%fused_computation.8.clone.1 | convolution fusion | flops 939655168 | bytes 8520704 | tf_op jit(solution)/shard_map/while/body/dot_general | solution.py:20
  343.9 5.5 %fusion.31 = bf16[384,1024]{1,0:T(8,128)(2,1)S(1)} fusion(bf16[384,1024]{1,0:T(8,128)(2,1)S(1)} %get-tuple-element.196, s32[]{:T(128)S(6)} %select_n.203, bf16[1024,3584]{1,0:T(8,128)(2,1)} %get-tuple-element.208, bf16[384,3584]{1,0:T(8,128)(2,1)S(1)} %get-tuple-element.207), kind=kOutput, calls=%fused_computation.8.clone.1 | convolution fusion | flops 939655168 | bytes 8520704 | tf_op jit(solution)/shard_map/while/body/dot_general | solution.py:20
  (42 shorter events, 18.1 us)
Async XLA Ops:
  10.3 10.2 %copy-start.6 = (bf16[512,8]{0,1:T(8,128)(2,1)S(1)}, bf16[512,8]{0,1:T(8,128)(2,1)}, u32[]{:S(2)}) copy-start(bf16[512,8]{0,1:T(8,128)(2,1)} %param.15) | copy-start | bytes 24580
  10.3 10.8 %copy-start.5 = (s32[512,8]{0,1:T(8,128)S(1)}, s32[512,8]{0,1:T(8,128)}, u32[]{:S(2)}) copy-start(s32[512,8]{0,1:T(8,128)} %param.14) | copy-start | bytes 49156
  10.3 10.9 %copy-start.7 = (s32[1,1,384]{2,1,0:T(1,128)S(1)}, s32[1,1,384]{2,1,0:T(1,128)}, u32[]{:S(2)}) copy-start(s32[1,1,384]{2,1,0:T(1,128)} %param.16) | copy-start | bytes 4612
  10.3 92.4 %all-to-all-start = ((bf16[16,512,224]{1,2,0:T(8,128)(2,1)}), bf16[16,512,224]{1,2,0:T(8,128)(2,1)}, u32[]{:S(2)}, u32[]{:S(2)}) async-start(bf16[16,512,224]{1,2,0:T(8,128)(2,1)} %stack.7), calls=%async_computation | async-start | bytes 7340032 | tf_op jit(solution)/shard_map/all_to_all | solution.py:42
  20.4 329.7 %reduce-scatter.4.cloned.1.call-start = ((), (), s32[]{:S(2)}) async-start(), calls=%async_computation.2 | async-start | bytes 7798784
  118.7 2.7 copy-start.3
  175.7 80.9 %collective-permute-start = (bf16[512,1792]{1,0:T(8,128)(2,1)}, bf16[512,1792]{1,0:T(8,128)(2,1)}, u32[]{:S(2)}, u32[]{:S(2)}) collective-permute-start(bf16[512,1792]{1,0:T(8,128)(2,1)} %select_convert_fusion), channel_id=1, source_target_pairs={{0,8},{1,9},{2,10},{3,11},{4,12},{5,13},{6,14},{7,15},{8,0},{9,1},... | collective-permute-start | bytes 5505032 | tf_op jit(solution)/shard_map/ppermute | solution.py:11
  260.8 1.9 copy-start
  263.9 41.3 %collective-permute-start.1 = (bf16[512,896]{1,0:T(8,128)(2,1)}, bf16[512,896]{1,0:T(8,128)(2,1)}, u32[]{:S(2)}, u32[]{:S(2)}) collective-permute-start(bf16[512,896]{1,0:T(8,128)(2,1)} %select_convert_fusion.1), channel_id=1, source_target_pairs={{0,4},{1,5},{2,6},{3,7},{4,0},{5,1},{6,2},{7,3},{8,12},{9,13},{10,... | collective-permute-start | bytes 2752520 | tf_op jit(solution)/shard_map/ppermute | solution.py:11
  307.7 1.3 copy-start.1
  309.2 13.4 %collective-permute-start.2 = (bf16[512,448]{1,0:T(8,128)(2,1)S(1)}, bf16[512,448]{1,0:T(8,128)(2,1)}, u32[]{:S(2)}, u32[]{:S(2)}) collective-permute-start(bf16[512,448]{1,0:T(8,128)(2,1)S(1)} %select_convert_fusion.2), channel_id=1, source_target_pairs={{0,2},{1,3},{2,0},{3,1},{4,6},{5,7},{6,4},{7,5},{8,10},{9,11},{10,... | collective-permute-start | bytes 1376264 | tf_op jit(solution)/shard_map/ppermute | solution.py:11
  324.7 1.0 copy-start.2
  325.8 2.6 collective-permute-start.3
  350.1 3.3 copy-start.4
Sparse Core Ops, SparseCore 0:
  137.7 86.9 reduce-scatter.3
